TPU v7x, 128 devices: a whole 4x4x4 slice. The times are simulated.
128 devices in a mesh: plane: 4 (over x_hi, core), ray: 32 (over z, y, x_lo).
Axes of the slice: x: 4 (x_hi: 2, x_lo: 2; x = x_hi * 2 + x_lo), y: 4, z: 4, core: 2. Of those that a mesh axis runs over, the one named last changes fastest.
Arguments:
- coarse_potential: float32 [2048, 512], P(('plane', 'ray')), may hold values from -72 to 72
- fine_tiles: bfloat16 [4, 32768, 256], P('plane', 'ray'), may hold values from -0.59765625 to 0.59765625
- tile_requests: int32 [128, 4, 32, 16], P(('plane', 'ray')), may hold values from 0 to 1023, as said below
- ray_slot: int32 [4, 131072], P(None, ('plane', 'ray')), may hold values from 0 to 511, as said below
- fine_cell: int32 [4, 131072], P(None, ('plane', 'ray')), may hold values from 17 to 221, as said below
- coarse_cell: int32 [4, 131072], P(None, ('plane', 'ray')), may hold values from 0 to 262143
- tile_root: int32 [4, 131072], P(None, ('plane', 'ray')), may hold values from 0 to 3
- ray_offset: float32 [2, 131072], P(None, ('plane', 'ray')), may hold values from 0 to 1
Outputs:
- displacement: float32 [2, 131072], P(None, ('plane', 'ray'))
- distortion: float32 [4, 131072], P(None, ('plane', 'ray'))
Inputs may be any that keep to these rules, and one draw needn't show every extreme that they name: `tile_requests`: entries are tile indices within one owner's tiles of the plane. `ray_slot`: A ray's slot r * 16 + s names a tile requested by its own bundle from owner r at that plane. `fine_cell`: both coordinates of a ray's fine cell lie in 1 to 13.
All inputs are finite; a program needn't handle non-finite values.
Results may differ from a plain program's by a relative error of at most 0.0026.
Values may be sent and summed in bfloat16 or wider, within the bound.
No kernel may reach another device: no remote copies, remote signals or barrier semaphores. Data moves between devices by JAX's collectives and lax.ppermute only.
A program may use at most 128 MiB of HBM per device.

v0:
```python
import jax
import jax.numpy as jnp
from jax import lax
from jax.sharding import PartitionSpec as P

TP = 16
RATIO = 32
FIRST = 31


def tile_fields(tiles):
    padded = jnp.pad(tiles, ((0, 0), (1, 1), (1, 1)))
    right_val = padded[:, 1:-1, 2:]
    left_val = padded[:, 1:-1, :-2]
    upper_val = padded[:, 2:, 1:-1]
    lower_val = padded[:, :-2, 1:-1]
    grad_x = (right_val - left_val) * 0.5
    grad_y = (upper_val - lower_val) * 0.5
    hess_xx = right_val - 2.0 * tiles + left_val
    hess_yy = upper_val - 2.0 * tiles + lower_val
    hess_xy = (
        padded[:, 2:, 2:] - padded[:, :-2, 2:] - padded[:, 2:, :-2] + padded[:, :-2, :-2]
    ) * 0.25
    return jnp.stack([grad_x, grad_y, hess_xx, hess_yy, hess_xy], axis=1)


def coarse_terms(plane_rows, coarse_row, fine_row, root_row, position, coarse_side):
    cell_x = coarse_row % coarse_side
    cell_y = coarse_row // coarse_side
    root_x = (root_row % 2 * (RATIO // 2)).astype(jnp.float32)
    root_y = (root_row // 2 * (RATIO // 2)).astype(jnp.float32)
    frac_x = (root_x + (fine_row % TP).astype(jnp.float32) + position[0]) / RATIO
    frac_y = (root_y + (fine_row // TP).astype(jnp.float32) + position[1]) / RATIO
    column_ids = jnp.arange(coarse_side, dtype=jnp.int32)[None, :]
    column_masks = [
        (column_ids == ((cell_x + shift_x) % coarse_side)[:, None]).astype(jnp.float32)
        for shift_x in range(-1, 3)
    ]
    grid_rows = []
    for shift_y in range(-1, 3):
        fetched = jnp.take(plane_rows, (cell_y + shift_y) % coarse_side, axis=0)
        grid_rows.append([jnp.sum(fetched * column_mask, axis=1) for column_mask in column_masks])
    weights = [
        (1.0 - frac_x) * (1.0 - frac_y),
        frac_x * (1.0 - frac_y),
        (1.0 - frac_x) * frac_y,
        frac_x * frac_y,
    ]
    total = jnp.zeros((5, coarse_row.shape[0]), jnp.float32)
    corner_list = ((0, 0), (0, 1), (1, 0), (1, 1))
    for corner_index in range(4):
        step_y = corner_list[corner_index][0] + 1
        step_x = corner_list[corner_index][1] + 1
        middle = grid_rows[step_y][step_x]
        right_val = grid_rows[step_y][step_x + 1]
        left_val = grid_rows[step_y][step_x - 1]
        upper_val = grid_rows[step_y + 1][step_x]
        lower_val = grid_rows[step_y - 1][step_x]
        cross = (
            grid_rows[step_y + 1][step_x + 1]
            - grid_rows[step_y - 1][step_x + 1]
            - grid_rows[step_y + 1][step_x - 1]
            + grid_rows[step_y - 1][step_x - 1]
        ) * 0.25
        stacked = jnp.stack(
            [
                (right_val - left_val) * 0.5,
                (upper_val - lower_val) * 0.5,
                right_val - 2.0 * middle + left_val,
                upper_val - 2.0 * middle + lower_val,
                cross,
            ]
        )
        total = total + weights[corner_index] * stacked
    scales = jnp.array(
        [
            1.0 / RATIO,
            1.0 / RATIO,
            1.0 / (RATIO * RATIO),
            1.0 / (RATIO * RATIO),
            1.0 / (RATIO * RATIO),
        ],
        jnp.float32,
    )
    return total * scales[:, None]


def advance(displacement, previous, distortion, before, deriv, plane_index):
    chi_now = float(FIRST + plane_index)
    ahead = 2.0 * chi_now / (chi_now + 1.0)
    behind = (chi_now - 1.0) / (chi_now + 1.0)
    strength = chi_now / (chi_now + 1.0)
    grad_x, grad_y, hess_xx, hess_yy, hess_xy = (deriv[0], deriv[1], deriv[2], deriv[3], deriv[4])
    new_disp = ahead * displacement - behind * previous - strength * jnp.stack([grad_x, grad_y])
    product = jnp.stack(
        [
            hess_xx * distortion[0] + hess_xy * distortion[2],
            hess_xx * distortion[1] + hess_xy * distortion[3],
            hess_xy * distortion[0] + hess_yy * distortion[2],
            hess_xy * distortion[1] + hess_yy * distortion[3],
        ]
    )
    new_dist = ahead * distortion - behind * before - strength * product
    return (new_disp, displacement, new_dist, distortion)


def fine_block(fields_flat, slot_row, cell_row, position):
    cand_count = fields_flat.shape[0]
    rows_here = slot_row.shape[0]
    tile_cells = TP * TP
    onehot = (slot_row[:, None] == jnp.arange(cand_count, dtype=jnp.int32)[None, :]).astype(
        jnp.bfloat16
    )
    picked = jnp.dot(onehot, fields_flat, preferred_element_type=jnp.float32).reshape(
        rows_here, 5, tile_cells
    )
    cell_ids = jnp.arange(tile_cells, dtype=jnp.int32)[None, :]
    along_x = position[0][:, None]
    along_y = position[1][:, None]
    anchor = cell_row[:, None]
    weights = (
        (1.0 - along_x) * (1.0 - along_y) * (cell_ids == anchor).astype(jnp.float32)
        + along_x * (1.0 - along_y) * (cell_ids == anchor + 1).astype(jnp.float32)
        + (1.0 - along_x) * along_y * (cell_ids == anchor + TP).astype(jnp.float32)
        + along_x * along_y * (cell_ids == anchor + TP + 1).astype(jnp.float32)
    )
    return jnp.einsum("bcn,bn->cb", picked, weights)


def body(
    coarse_potential,
    fine_tiles,
    tile_requests,
    ray_slot,
    fine_cell,
    coarse_cell,
    tile_root,
    ray_offset,
):
    planes = lax.axis_size("plane")
    owners = lax.axis_size("ray")
    slot_count = tile_requests.shape[3]
    coarse_side = coarse_potential.shape[1]
    count_rays = ray_offset.shape[1]
    tile_cells = TP * TP
    requests_local = tile_requests.reshape(planes, owners, slot_count)
    wanted_ids = lax.all_to_all(
        requests_local.reshape(planes * owners, slot_count),
        ("plane", "ray"),
        split_axis=0,
        concat_axis=0,
        tiled=True,
    )
    outgoing = jnp.take(fine_tiles[0], wanted_ids.reshape(-1), axis=0).reshape(
        planes, owners, slot_count, tile_cells
    )
    arrived = lax.all_to_all(
        outgoing.reshape(planes * owners, slot_count, tile_cells),
        ("plane", "ray"),
        split_axis=0,
        concat_axis=0,
        tiled=True,
    )
    arrived = arrived.reshape(planes, owners * slot_count, TP, TP)
    whole_rows = lax.all_gather(coarse_potential, ("plane", "ray"), axis=0, tiled=True)
    displacement = jnp.zeros((2, count_rays), jnp.float32)
    previous = displacement
    ones_row = jnp.ones((count_rays,), jnp.float32)
    zero_row = jnp.zeros((count_rays,), jnp.float32)
    distortion = jnp.stack([ones_row, zero_row, zero_row, ones_row])
    before = distortion
    block_rows = min(512, count_rays)
    block_total = count_rays // block_rows
    for plane_index in range(planes):
        position = ray_offset + displacement
        plane_rows = whole_rows[plane_index * coarse_side : (plane_index + 1) * coarse_side]
        coarse_part = coarse_terms(
            plane_rows,
            coarse_cell[plane_index],
            fine_cell[plane_index],
            tile_root[plane_index],
            position,
            coarse_side,
        )
        fields_flat = (
            tile_fields(arrived[plane_index].astype(jnp.float32))
            .astype(jnp.bfloat16)
            .reshape(-1, 5 * tile_cells)
        )

        def run_block(pieces):
            return fine_block(fields_flat, pieces[0], pieces[1], pieces[2])

        fine_blocks = lax.map(
            run_block,
            (
                ray_slot[plane_index].reshape(block_total, block_rows),
                fine_cell[plane_index].reshape(block_total, block_rows),
                position.reshape(2, block_total, block_rows).transpose(1, 0, 2),
            ),
        )
        fine_part = fine_blocks.transpose(1, 0, 2).reshape(5, count_rays)
        displacement, previous, distortion, before = advance(
            displacement, previous, distortion, before, fine_part + coarse_part, plane_index
        )
    return (displacement, distortion)


def solution(mesh):
    in_specs = (
        P(("plane", "ray"), None),
        P("plane", "ray", None),
        P(("plane", "ray"), None, None, None),
        P(None, ("plane", "ray")),
        P(None, ("plane", "ray")),
        P(None, ("plane", "ray")),
        P(None, ("plane", "ray")),
        P(None, ("plane", "ray")),
    )
    out_specs = (P(None, ("plane", "ray")), P(None, ("plane", "ray")))
    return jax.shard_map(body, mesh=mesh, in_specs=in_specs, out_specs=out_specs, check_vma=False)
```

profile of v0, /device:TPU:1, one launch (start us, length us, event | category | flops | bytes accessed | tf_op | source)
XLA Modules:
  0.0 516.5 jit_solution(14348921904441071178)
XLA Ops:
  8.7 11.5 %all-to-all-start = ((s32[128,1,16]{2,1,0:T(1,128)}), s32[128,1,16]{2,1,0:T(1,128)S(1)}, u32[]{:S(2)}, u32[]{:S(2)}) async-start(s32[128,1,16]{2,1,0:T(1,128)} %bitcast.38), calls=%async_computation | async-start | bytes 131072 | tf_op jit(solution)/shard_map/all_to_all | solution.py:147
  31.3 7.5 %gather_fusion = bf16[2048,256]{1,0:T(8,128)(2,1)S(1)} fusion(bf16[1024,256]{1,0:T(8,128)(2,1)S(1)} %bitcast.261, s32[2048]{0:T(1024)S(1)} %broadcast_clamp_fusion), kind=kCustom, calls=%fused_computation.16 | custom fusion | bytes 2105344 | tf_op jit(solution)/shard_map/jit(_take)/gather | solution.py:154
  40.1 9.5 %all-to-all-start.1 = ((bf16[128,16,256]{2,1,0:T(8,128)(2,1)}), bf16[128,16,256]{2,1,0:T(8,128)(2,1)S(1)}, u32[]{:S(2)}, u32[]{:S(2)}) async-start(bf16[128,16,256]{2,1,0:T(8,128)(2,1)} %broadcast_select_fusion), calls=%async_computation.1 | async-start | bytes 2097152 | tf_op jit(solution)/shard_map/all_to_all | solution.py:157
  52.3 17.2 %all-to-all-done.1 = bf16[128,16,256]{2,1,0:T(8,128)(2,1)S(1)} async-done(((bf16[128,16,256]{2,1,0:T(8,128)(2,1)}), bf16[128,16,256]{2,1,0:T(8,128)(2,1)S(1)}, u32[]{:S(2)}, u32[]{:S(2)}) %all-to-all-start.1) | async-done | bytes 1048608 | tf_op jit(solution)/shard_map/all_to_all | solution.py:157
  70.5 2.7 reshape.2442
  73.2 31.9 %fusion.47 = (bf16[512,1,16,16]{3,2,0,1:T(8,128)(2,1)S(1)}, bf16[512,1,16,16]{3,2,0,1:T(8,128)(2,1)}, bf16[512,1,16,16]{3,2,0,1:T(8,128)(2,1)}, bf16[512,1,16,16]{3,2,0,1:T(8,128)(2,1)}, bf16[512,1,16,16]{3,2,0,1:T(8,128)(2,1)}) fusion(f32[512,16,16]{2,1,0:T(8,128)} %reshape.2442), kind=kLoop, calls=%fused_computation.264 | loop fusion | flops 2359296 | bytes 1835008 | tf_op jit(solution)/shard_map/stack | solution.py:24
  108.3 3.1 copy.57
  111.4 3.1 copy.58
  127.6 2.6 reshape.2443
  130.2 32.1 %fusion.46 = (bf16[512,1,16,16]{3,2,0,1:T(8,128)(2,1)S(1)}, bf16[512,1,16,16]{3,2,0,1:T(8,128)(2,1)}, bf16[512,1,16,16]{3,2,0,1:T(8,128)(2,1)}, bf16[512,1,16,16]{3,2,0,1:T(8,128)(2,1)}, bf16[512,1,16,16]{3,2,0,1:T(8,128)(2,1)}) fusion(f32[512,16,16]{2,1,0:T(8,128)} %reshape.2443), kind=kLoop, calls=%fused_computation.263 | loop fusion | flops 2359296 | bytes 1835008 | tf_op jit(solution)/shard_map/stack | solution.py:24
  162.3 3.1 copy.64
  165.4 3.1 copy.65
  168.5 3.1 copy.66
  180.9 2.6 reshape.2444
  183.5 31.9 %fusion.45 = (bf16[512,1,16,16]{3,2,0,1:T(8,128)(2,1)S(1)}, bf16[512,1,16,16]{3,2,0,1:T(8,128)(2,1)}, bf16[512,1,16,16]{3,2,0,1:T(8,128)(2,1)}, bf16[512,1,16,16]{3,2,0,1:T(8,128)(2,1)}, bf16[512,1,16,16]{3,2,0,1:T(8,128)(2,1)}) fusion(f32[512,16,16]{2,1,0:T(8,128)} %reshape.2444), kind=kLoop, calls=%fused_computation.262 | loop fusion | flops 2359296 | bytes 1835008 | tf_op jit(solution)/shard_map/stack | solution.py:24
  215.5 3.1 copy.72
  218.6 3.3 copy.73
  234.6 31.9 %fusion.44 = (bf16[512,1,16,16]{3,2,0,1:T(8,128)(2,1)S(1)}, bf16[512,1,16,16]{3,2,0,1:T(8,128)(2,1)}, bf16[512,1,16,16]{3,2,0,1:T(8,128)(2,1)}, bf16[512,1,16,16]{3,2,0,1:T(8,128)(2,1)}, bf16[512,1,16,16]{3,2,0,1:T(8,128)(2,1)}) fusion(f32[512,16,16]{2,1,0:T(8,128)} %reshape.2445), kind=kLoop, calls=%fused_computation.261 | loop fusion | flops 2359296 | bytes 1835008 | tf_op jit(solution)/shard_map/stack | solution.py:24
  279.7 11.4 %while.48 = (s32[]{:T(128)}, f32[2,5,512]{2,1,0:T(8,128)S(1)}, s32[2,512]{1,0:T(2,128)S(1)}, f32[2,2,512]{2,1,0:T(2,128)S(1)}, s32[2,512]{1,0:T(2,128)S(1)}, /*i...) while((s32[]{:T(128)}, f32[2,5,512]{2,1,0:T(8,128)S(1)}, s32[2,512]{1,0:T(2,128)S(1)}, ...), condition=%wide.region_1.2_spmd, body=%wide.region_0.1_spmd.sunk | while | flops 674105344 | bytes 8749185 | solution.py:194
  291.1 39.7 %all-gather.2.cloned.1.call-done = f32[2048,512]{1,0:T(8,128)} async-done(((f32[16,512]{1,0:T(8,128)}), f32[2048,512]{1,0:T(8,128)}) %all-gather.2.cloned.1.call-update) | async-done | bytes 4194320 | tf_op jit(solution)/shard_map/all_gather | solution.py:165
  330.9 3.6 fusion.134
  334.4 6.5 %gather_fusion.2 = f32[1024,512]{1,0:T(8,128)} fusion(f32[512,512]{1,0:T(8,128)} %get-tuple-element.600, s32[1024]{0:T(1024)S(1)} %get-tuple-element.791), kind=kCustom, calls=%fused_computation.1.clone | custom fusion | bytes 4198400 | tf_op jit(solution)/shard_map/jit(_take)/gather | solution.py:41
  340.9 6.5 %gather_fusion.3 = f32[1024,512]{1,0:T(8,128)} fusion(f32[512,512]{1,0:T(8,128)} %get-tuple-element.600, s32[1024]{0:T(1024)S(1)} %get-tuple-element.790), kind=kCustom, calls=%fused_computation.2.clone | custom fusion | bytes 4198400 | tf_op jit(solution)/shard_map/jit(_take)/gather | solution.py:41
  347.5 6.5 %gather_fusion.4 = f32[1024,512]{1,0:T(8,128)} fusion(f32[512,512]{1,0:T(8,128)} %get-tuple-element.600, s32[1024]{0:T(1024)S(1)} %get-tuple-element.789), kind=kCustom, calls=%fused_computation.3.clone | custom fusion | bytes 4198400 | tf_op jit(solution)/shard_map/jit(_take)/gather | solution.py:41
  354.0 6.5 %gather_fusion.1 = f32[1024,512]{1,0:T(8,128)} fusion(f32[512,512]{1,0:T(8,128)} %get-tuple-element.600, s32[1024]{0:T(1024)S(1)} %get-tuple-element.792), kind=kCustom, calls=%fused_computation.clone | custom fusion | bytes 4198400 | tf_op jit(solution)/shard_map/jit(_take)/gather | solution.py:41
  360.6 9.5 %select_reduce_fusion.56 = (f32[1024]{0:T(1024)S(1)}, f32[1024]{0:T(1024)S(1)}, f32[1024]{0:T(1024)S(1)}, f32[1024]{0:T(1024)S(1)}, f32[1024]{0:T(1024)S(1)}, /*...) fusion(f32[1024,512]{1,0:T(8,128)} %gather_fusion.2, ...), kind=kLoop, calls=%fused_computation.250 | loop fusion | flops 20955136 | bytes 8474624 | tf_op jit(solution)/shard_map/reduce_sum | solution.py:42
  371.9 19.3 %while.49 = (s32[]{:T(128)}, f32[2,5,512]{2,1,0:T(8,128)S(1)}, s32[2,512]{1,0:T(2,128)S(1)}, f32[2,2,512]{2,1,0:T(2,128)S(1)}, s32[2,512]{1,0:T(2,128)S(1)}, /*i...) while((s32[]{:T(128)}, f32[2,5,512]{2,1,0:T(8,128)S(1)}, s32[2,512]{1,0:T(2,128)S(1)}, ...), condition=%wide.region_19.21_spmd, body=%wide.region_18.20_spmd.sunk | while | flops 674105344 | bytes 8749185 | solution.py:194
  371.9 3.9 fusion.151
  381.6 3.9 fusion.151
  391.2 4.9 gather_fusion.6
  396.1 4.9 gather_fusion.7
  401.0 4.9 gather_fusion.8
  405.9 4.9 gather_fusion.5
  410.9 9.5 %select_reduce_fusion.40 = (f32[1024]{0:T(1024)S(1)}, f32[1024]{0:T(1024)S(1)}, f32[1024]{0:T(1024)S(1)}, f32[1024]{0:T(1024)S(1)}, f32[1024]{0:T(1024)S(1)}, /*...) fusion(f32[1024,512]{1,0:T(8,128)} %gather_fusion.6, ...), kind=kLoop, calls=%fused_computation.230 | loop fusion | flops 20955136 | bytes 8474624 | tf_op jit(solution)/shard_map/reduce_sum | solution.py:42
  421.5 14.0 %while.50 = (s32[]{:T(128)}, f32[2,5,512]{2,1,0:T(8,128)S(1)}, s32[2,512]{1,0:T(2,128)S(1)}, f32[2,2,512]{2,1,0:T(2,128)S(1)}, s32[2,512]{1,0:T(2,128)S(1)}, /*i...) while((s32[]{:T(128)}, f32[2,5,512]{2,1,0:T(8,128)S(1)}, s32[2,512]{1,0:T(2,128)S(1)}, ...), condition=%wide.region_37.39_spmd, body=%wide.region_36.38_spmd.sunk | while | flops 674105344 | bytes 8749185 | solution.py:194
  421.6 3.9 fusion.153
  428.5 3.9 fusion.153
  435.4 4.9 gather_fusion.10
  440.3 4.9 gather_fusion.11
  445.2 4.9 gather_fusion.12
  450.2 4.9 gather_fusion.9
  455.2 9.6 %select_reduce_fusion.24 = (f32[1024]{0:T(1024)S(1)}, f32[1024]{0:T(1024)S(1)}, f32[1024]{0:T(1024)S(1)}, f32[1024]{0:T(1024)S(1)}, f32[1024]{0:T(1024)S(1)}, /*...) fusion(f32[1024,512]{1,0:T(8,128)} %gather_fusion.10, ...), kind=kLoop, calls=%fused_computation.210 | loop fusion | flops 20955136 | bytes 8474624 | tf_op jit(solution)/shard_map/reduce_sum | solution.py:42
  467.3 12.5 %while.51 = (s32[]{:T(128)}, f32[2,5,512]{2,1,0:T(8,128)S(1)}, s32[2,512]{1,0:T(2,128)}, f32[2,2,512]{2,1,0:T(2,128)S(1)}, s32[2,512]{1,0:T(2,128)}, /*index=5*/...) while((s32[]{:T(128)}, f32[2,5,512]{2,1,0:T(8,128)S(1)}, s32[2,512]{1,0:T(2,128)}, ...), condition=%wide.region_55.57_spmd, body=%wide.region_54.56_spmd.sunk | while | flops 674105344 | bytes 8749185 | solution.py:194
  479.8 3.5 gather_fusion.14
  483.3 4.9 gather_fusion.15
  488.2 4.9 gather_fusion.16
  493.3 4.9 gather_fusion.13
  498.6 9.2 %select_reduce_fusion.8 = (f32[1024]{0:T(1024)S(1)}, f32[1024]{0:T(1024)S(1)}, f32[1024]{0:T(1024)S(1)}, f32[1024]{0:T(1024)S(1)}, f32[1024]{0:T(1024)S(1)}, /*i...) fusion(f32[1024,512]{1,0:T(8,128)S(1)} %gather_fusion.14, ...), kind=kLoop, calls=%fused_computation.190 | loop fusion | flops 20955136 | bytes 8474624 | tf_op jit(solution)/shard_map/reduce_sum | solution.py:42
  (294 shorter events, 116.7 us)
Async XLA Ops:
  7.2 24.1 %copy-start = (bf16[1,1024,256]{2,1,0:T(8,128)(2,1)S(1)}, bf16[1,1024,256]{2,1,0:T(8,128)(2,1)}, u32[]{:S(2)}) copy-start(bf16[1,1024,256]{2,1,0:T(8,128)(2,1)} %param.23) | copy-start | bytes 1572868
  8.7 21.1 %all-to-all-start = ((s32[128,1,16]{2,1,0:T(1,128)}), s32[128,1,16]{2,1,0:T(1,128)S(1)}, u32[]{:S(2)}, u32[]{:S(2)}) async-start(s32[128,1,16]{2,1,0:T(1,128)} %bitcast.38), calls=%async_computation | async-start | bytes 131072 | tf_op jit(solution)/shard_map/all_to_all | solution.py:147
  20.2 310.6 %all-gather.2.cloned.1.call-start = ((), (), s32[]{:S(2)}) async-start(), calls=%async_computation.2 | async-start | bytes 4227072 | tf_op jit(solution)/shard_map/all_gather | solution.py:165
  38.8 11.4 %copy-start.5 = (f32[2,1024]{1,0:T(2,128)S(1)}, f32[2,1024]{1,0:T(2,128)}, u32[]{:S(2)}) copy-start(f32[2,1024]{1,0:T(2,128)} %param.29) | copy-start | bytes 24580
  38.8 11.4 %copy-start.11 = (s32[4,1024]{1,0:T(4,128)S(1)}, s32[4,1024]{1,0:T(4,128)}, u32[]{:S(2)}) copy-start(s32[4,1024]{1,0:T(4,128)} %param.26) | copy-start | bytes 49156
  40.1 29.4 %all-to-all-start.1 = ((bf16[128,16,256]{2,1,0:T(8,128)(2,1)}), bf16[128,16,256]{2,1,0:T(8,128)(2,1)S(1)}, u32[]{:S(2)}, u32[]{:S(2)}) async-start(bf16[128,16,256]{2,1,0:T(8,128)(2,1)} %broadcast_select_fusion), calls=%async_computation.1 | async-start | bytes 2097152 | tf_op jit(solution)/shard_map/all_to_all | solution.py:157
  121.0 6.6 %copy-start.2 = (f32[32,16,256]{2,1,0:T(8,128)S(1)}, f32[32,16,256]{2,1,0:T(8,128)}, u32[]{:S(2)}) copy-start(f32[32,16,256]{2,1,0:T(8,128)} %get-tuple-element.623) | copy-start | bytes 1572868
  354.0 6.5 %copy-start.48 = (pred[1024]{0:T(1024)(128)(4,1)S(1)}, pred[1024]{0:T(1024)(128)(4,1)}, u32[]{:S(2)}) copy-start(pred[1024]{0:T(1024)(128)(4,1)} %get-tuple-element.551) | copy-start | bytes 3076
  354.0 6.5 %copy-start.49 = (pred[1024]{0:T(1024)(128)(4,1)S(1)}, pred[1024]{0:T(1024)(128)(4,1)}, u32[]{:S(2)}) copy-start(pred[1024]{0:T(1024)(128)(4,1)} %get-tuple-element.774) | copy-start | bytes 3076
  354.0 6.5 %copy-start.50 = (pred[1024]{0:T(1024)(128)(4,1)S(1)}, pred[1024]{0:T(1024)(128)(4,1)}, u32[]{:S(2)}) copy-start(pred[1024]{0:T(1024)(128)(4,1)} %get-tuple-element.775) | copy-start | bytes 3076
  354.0 6.5 %copy-start.51 = (pred[1024]{0:T(1024)(128)(4,1)S(1)}, pred[1024]{0:T(1024)(128)(4,1)}, u32[]{:S(2)}) copy-start(pred[1024]{0:T(1024)(128)(4,1)} %get-tuple-element.776) | copy-start | bytes 3076
  360.6 9.8 %copy-start.30 = (f32[1,1024]{1,0:T(1,128)S(1)}, f32[1,1024]{1,0:T(1,128)}, u32[]{:S(2)}) copy-start(f32[1,1024]{1,0:T(1,128)} %get-tuple-element.714) | copy-start | bytes 12292
  360.6 11.2 %copy-start.26 = (s32[4,1024]{1,0:T(4,128)S(1)}, s32[4,1024]{1,0:T(4,128)}, u32[]{:S(2)}) copy-start(s32[4,1024]{1,0:T(4,128)} %param.28) | copy-start | bytes 49156
  405.9 4.9 copy-start.46
  405.9 5.0 copy-start.47
  410.9 9.8 %copy-start.33 = (f32[5]{0:T(128)S(1)}, f32[5]{0:T(128)}, u32[]{:S(2)}) copy-start(f32[5]{0:T(128)} %constant.668.clone) | copy-start | bytes 64
  450.1 5.0 copy-start.21
  450.1 5.0 copy-start.22
  450.1 5.0 copy-start.23
  450.1 5.0 copy-start.24
  450.2 5.0 copy-start.40
  450.2 5.0 copy-start.41
  450.2 5.0 copy-start.42
  450.2 5.0 copy-start.43
  455.2 9.9 %copy-start.32 = (f32[1,1024]{1,0:T(1,128)S(1)}, f32[1,1024]{1,0:T(1,128)}, u32[]{:S(2)}) copy-start(f32[1,1024]{1,0:T(1,128)} %get-tuple-element.538) | copy-start | bytes 12292
  455.2 9.9 %copy-start.34 = (f32[5]{0:T(128)S(1)}, f32[5]{0:T(128)}, u32[]{:S(2)}) copy-start(f32[5]{0:T(128)} %constant.668.clone) | copy-start | bytes 64
  455.2 12.0 %copy-start.3 = (bf16[512,1280]{1,0:T(8,128)(2,1)S(1)}, bf16[512,1280]{1,0:T(8,128)(2,1)}, u32[]{:S(2)}) copy-start(bf16[512,1280]{1,0:T(8,128)(2,1)} %copy.85) | copy-start | bytes 3932164
  467.2 12.6 %copy-start.20 = (s32[1024]{0:T(1024)S(1)}, s32[1024]{0:T(1024)}, u32[]{:S(2)}) copy-start(s32[1024]{0:T(1024)} %get-tuple-element.738) | copy-start | bytes 12292
  493.2 5.1 copy-start.6
  493.2 5.1 copy-start.7
  493.2 5.1 copy-start.8
  493.2 5.0 copy-start.9
  493.2 5.0 copy-start.10
  493.2 5.1 copy-start.27
  493.2 5.2 %copy-start.28 = (f32[1,1024]{1,0:T(1,128)S(1)}, f32[1,1024]{1,0:T(1,128)}, u32[]{:S(2)}) copy-start(f32[1,1024]{1,0:T(1,128)} %get-tuple-element.532) | copy-start | bytes 12292
  493.2 5.2 %copy-start.29 = (f32[1,1024]{1,0:T(1,128)S(1)}, f32[1,1024]{1,0:T(1,128)}, u32[]{:S(2)}) copy-start(f32[1,1024]{1,0:T(1,128)} %get-tuple-element.533) | copy-start | bytes 12292
  493.2 5.2 %copy-start.13 = (s32[1024]{0:T(1024)S(1)}, s32[1024]{0:T(1024)}, u32[]{:S(2)}) copy-start(s32[1024]{0:T(1024)} %get-tuple-element.744) | copy-start | bytes 12292
  493.2 5.2 %copy-start.14 = (s32[1024]{0:T(1024)S(1)}, s32[1024]{0:T(1024)}, u32[]{:S(2)}) copy-start(s32[1024]{0:T(1024)} %get-tuple-element.745) | copy-start | bytes 12292
  493.3 5.2 %copy-start.15 = (s32[1024]{0:T(1024)S(1)}, s32[1024]{0:T(1024)}, u32[]{:S(2)}) copy-start(s32[1024]{0:T(1024)} %get-tuple-element.746) | copy-start | bytes 12292
  493.3 5.2 %copy-start.16 = (s32[1024]{0:T(1024)S(1)}, s32[1024]{0:T(1024)}, u32[]{:S(2)}) copy-start(s32[1024]{0:T(1024)} %get-tuple-element.747) | copy-start | bytes 12292
  493.3 5.2 %copy-start.36 = (pred[1024]{0:T(1024)(128)(4,1)S(1)}, pred[1024]{0:T(1024)(128)(4,1)}, u32[]{:S(2)}) copy-start(pred[1024]{0:T(1024)(128)(4,1)} %get-tuple-element.534) | copy-start | bytes 3076
  493.3 5.2 %copy-start.37 = (pred[1024]{0:T(1024)(128)(4,1)S(1)}, pred[1024]{0:T(1024)(128)(4,1)}, u32[]{:S(2)}) copy-start(pred[1024]{0:T(1024)(128)(4,1)} %get-tuple-element.741) | copy-start | bytes 3076
  493.3 5.2 %copy-start.38 = (pred[1024]{0:T(1024)(128)(4,1)S(1)}, pred[1024]{0:T(1024)(128)(4,1)}, u32[]{:S(2)}) copy-start(pred[1024]{0:T(1024)(128)(4,1)} %get-tuple-element.742) | copy-start | bytes 3076
  493.3 5.2 %copy-start.39 = (pred[1024]{0:T(1024)(128)(4,1)S(1)}, pred[1024]{0:T(1024)(128)(4,1)}, u32[]{:S(2)}) copy-start(pred[1024]{0:T(1024)(128)(4,1)} %get-tuple-element.743) | copy-start | bytes 3076
  498.5 9.5 %copy-start.31 = (f32[1,1024]{1,0:T(1,128)S(1)}, f32[1,1024]{1,0:T(1,128)}, u32[]{:S(2)}) copy-start(f32[1,1024]{1,0:T(1,128)} %get-tuple-element.531) | copy-start | bytes 12292
  498.5 9.5 %copy-start.35 = (f32[5]{0:T(128)S(1)}, f32[5]{0:T(128)}, u32[]{:S(2)}) copy-start(f32[5]{0:T(128)} %constant.668.clone) | copy-start | bytes 64
  498.6 9.6 %copy-start.12 = (f32[2,1024]{1,0:T(2,128)S(1)}, f32[2,1024]{1,0:T(2,128)}, u32[]{:S(2)}) copy-start(f32[2,1024]{1,0:T(2,128)} %get-tuple-element.537) | copy-start | bytes 24580
  498.6 10.9 %copy-start.1 = (bf16[1,1024,256]{2,1,0:T(8,128)(2,1)S(1)}, bf16[1,1024,256]{2,1,0:T(8,128)(2,1)}, u32[]{:S(2)}) copy-start(bf16[1,1024,256]{2,1,0:T(8,128)(2,1)} %param.23) | copy-start | bytes 1572868
  (7 other events, 31.1 us)
Sparse Core Ops, SparseCore 0:
  22.7 308.0 all-gather.1
where the time goes:
time: 527 us; the launch traced here: 517 us
  other arithmetic  206 us (39%)
  local copies, waits for them, and re-layouts  190 us (36%)
  waiting for transfers between devices  57.8 us (11%)
  matrix products  25.3 us (5%)
  starting transfers between devices  21.1 us (4%)
  between operations  15.2 us (3%)
    another operation x4, other arithmetic, tile_fields(): return jnp.stack([grad_x, grad_y, hess_xx, hess_yy, hess_xy], axis=1)  128 us
    gather x16, local copies, waits for them, and re-layouts, coarse_terms(): fetched = jnp.take(plane_rows, (cell_y + shift_y) % coarse_side, axis=0)  83.5 us
    another operation x24, local copies, waits for them, and re-layouts, tile_fields(): return jnp.stack([grad_x, grad_y, hess_xx, hess_yy, hess_xy], axis=1)  53.9 us
    all_gather x1, waiting for transfers between devices, body(): lax.all_gather(coarse_potential, ('plane', 'ray'), axis=0, tiled=True)  39.7 us
    reduce_sum x4, other arithmetic, coarse_terms(): jnp.sum(fetched * column_mask, axis=1)  37.7 us
    dot_general x8, matrix products, fine_block(): jnp.dot(onehot, fields_flat, preferred_element_type=jnp.float32)  25.3 us
    all_to_all x1, waiting for transfers between devices, body(): lax.all_to_all(outgoing.reshape(planes * owners, slot_count, tile_cells),...  17.2 us
    dot_general x8, other arithmetic, fine_block(): return jnp.einsum('bcn,bn->cb', picked, weights)  15.8 us
  transfers between devices with their start and end apart: 3, of which 3 were waited for; matrix products, arithmetic and copies ran while one was open for 47% of the time, Pallas kernels for 0%

commit v1 on v0

--- a/solution.py
+++ b/solution.py
@@ -6,6 +6,13 @@
 TP = 16
 RATIO = 32
 FIRST = 31
+
+
+def exchange_gather(value, axis, d):
+    size = lax.axis_size(axis)
+    shards = jnp.stack([value for _ in range(size)])
+    shards = lax.all_to_all(shards, axis, split_axis=0, concat_axis=0)
+    return jnp.concatenate(shards, axis=d)
 
 
 def tile_fields(tiles):
@@ -162,7 +169,7 @@
         tiled=True,
     )
     arrived = arrived.reshape(planes, owners * slot_count, TP, TP)
-    whole_rows = lax.all_gather(coarse_potential, ("plane", "ray"), axis=0, tiled=True)
+    whole_rows = exchange_gather(coarse_potential, ("plane", "ray"), 0)
     displacement = jnp.zeros((2, count_rays), jnp.float32)
     previous = displacement
     ones_row = jnp.ones((count_rays,), jnp.float32)

time: 527 us -> 493 us (0.935)
  waiting for transfers between devices: 57.8 us -> 15.8 us
  between operations: 15.2 us -> 2.01 us
  local copies, waits for them, and re-layouts: 190 us -> 201 us
  other arithmetic: 206 us -> 216 us
  starting transfers between devices: 21.1 us -> 26.8 us
    all_gather x1 -> x0, waiting for transfers between devices: 39.7 us -> none  [body(): lax.all_gather(coarse_potential, ('plane', 'ray'), axis=0, tiled=True)]
    another operation x4, other arithmetic: 128 us -> 136 us  [tile_fields(): return jnp.stack([grad_x, grad_y, hess_xx, hess_yy, hess_xy], axis=1)]
    all_to_all x0 -> x1, starting transfers between devices: none -> 5.93 us  [exchange_gather(): shards = lax.all_to_all(shards, axis, split_axis=0, concat_axis=0)]
    unnamed x120 -> x146, local copies, waits for them, and re-layouts: 10.1 us -> 13.7 us
  transfers between devices with their start and end apart: 3 -> 3, of which waited for: 3 -> 2; matrix products, arithmetic and copies ran while one was open for 47% -> 51% of each run, Pallas kernels for 0% -> 0%
where the time goes in v1:
time: 493 us; the launch traced here: 487 us
  other arithmetic  216 us (44%)
  local copies, waits for them, and re-layouts  201 us (41%)
  starting transfers between devices  26.8 us (5%)
  matrix products  25.3 us (5%)
  waiting for transfers between devices  15.8 us (3%)
    another operation x4, other arithmetic, tile_fields(): return jnp.stack([grad_x, grad_y, hess_xx, hess_yy, hess_xy], axis=1)  136 us
    gather x16, local copies, waits for them, and re-layouts, coarse_terms(): fetched = jnp.take(plane_rows, (cell_y + shift_y) % coarse_side, axis=0)  83.5 us
    another operation x24, local copies, waits for them, and re-layouts, tile_fields(): return jnp.stack([grad_x, grad_y, hess_xx, hess_yy, hess_xy], axis=1)  57.1 us
    reduce_sum x4, other arithmetic, coarse_terms(): jnp.sum(fetched * column_mask, axis=1)  37.8 us
    dot_general x8, matrix products, fine_block(): jnp.dot(onehot, fields_flat, preferred_element_type=jnp.float32)  25.3 us
    dot_general x8, other arithmetic, fine_block(): return jnp.einsum('bcn,bn->cb', picked, weights)  15.8 us
    all_to_all x1, waiting for transfers between devices, body(): lax.all_to_all(outgoing.reshape(planes * owners, slot_count, tile_cells),...  15.4 us
    unnamed x146, local copies, waits for them, and re-layouts  13.7 us
  transfers between devices with their start and end apart: 3, of which 2 were waited for; matrix products, arithmetic and copies ran while one was open for 51% of the time, Pallas kernels for 0%

profile of v1, /device:TPU:1, one launch (start us, length us, event | category | flops | bytes accessed | tf_op | source)
XLA Modules:
  0.0 487.1 jit_solution(8249550944642795958)
XLA Ops:
  2.2 11.5 %all-to-all-start = ((s32[128,1,16]{2,1,0:T(1,128)}), s32[128,1,16]{2,1,0:T(1,128)S(1)}, u32[]{:S(2)}, u32[]{:S(2)}) async-start(s32[128,1,16]{2,1,0:T(1,128)} %bitcast.38), calls=%async_computation | async-start | bytes 131072 | tf_op jit(solution)/shard_map/all_to_all | solution.py:154
  24.8 7.5 %gather_fusion = bf16[2048,256]{1,0:T(8,128)(2,1)S(1)} fusion(bf16[1024,256]{1,0:T(8,128)(2,1)S(1)} %bitcast.265, s32[2048]{0:T(1024)S(1)} %broadcast_clamp_fusion), kind=kCustom, calls=%fused_computation.16 | custom fusion | bytes 2105344 | tf_op jit(solution)/shard_map/jit(_take)/gather | solution.py:161
  33.5 9.4 %all-to-all-start.1 = ((bf16[128,16,256]{2,1,0:T(8,128)(2,1)}), bf16[128,16,256]{2,1,0:T(8,128)(2,1)S(1)}, u32[]{:S(2)}, u32[]{:S(2)}) async-start(bf16[128,16,256]{2,1,0:T(8,128)(2,1)} %broadcast_select_fusion), calls=%async_computation.1 | async-start | bytes 2097152 | tf_op jit(solution)/shard_map/all_to_all | solution.py:164
  46.8 15.4 %all-to-all-done.1 = bf16[128,16,256]{2,1,0:T(8,128)(2,1)S(1)} async-done(((bf16[128,16,256]{2,1,0:T(8,128)(2,1)}), bf16[128,16,256]{2,1,0:T(8,128)(2,1)S(1)}, u32[]{:S(2)}, u32[]{:S(2)}) %all-to-all-start.1) | async-done | bytes 1048608 | tf_op jit(solution)/shard_map/all_to_all | solution.py:164
  64.7 5.9 %all-to-all-start.2 = ((f32[128,16,512]{2,1,0:T(8,128)}), f32[128,16,512]{2,1,0:T(8,128)}, u32[]{:S(2)}, u32[]{:S(2)}) async-start(f32[128,16,512]{2,1,0:T(8,128)} %stack.128), calls=%async_computation.2 | async-start | bytes 8388608 | tf_op jit(solution)/shard_map/all_to_all | solution.py:14
  74.3 33.9 %fusion.47 = (bf16[512,1,16,16]{3,2,0,1:T(8,128)(2,1)S(1)}, bf16[512,1,16,16]{3,2,0,1:T(8,128)(2,1)}, bf16[512,1,16,16]{3,2,0,1:T(8,128)(2,1)}, bf16[512,1,16,16]{3,2,0,1:T(8,128)(2,1)}, bf16[512,1,16,16]{3,2,0,1:T(8,128)(2,1)}) fusion(f32[512,16,16]{2,1,0:T(8,128)} %reshape.2449), kind=kLoop, calls=%fused_computation.264 | loop fusion | flops 2359296 | bytes 1835008 | tf_op jit(solution)/shard_map/stack | solution.py:31
  111.4 3.1 copy.57
  114.6 3.1 copy.58
  130.7 2.6 reshape.2450
  133.3 33.9 %fusion.46 = (bf16[512,1,16,16]{3,2,0,1:T(8,128)(2,1)S(1)}, bf16[512,1,16,16]{3,2,0,1:T(8,128)(2,1)}, bf16[512,1,16,16]{3,2,0,1:T(8,128)(2,1)}, bf16[512,1,16,16]{3,2,0,1:T(8,128)(2,1)}, bf16[512,1,16,16]{3,2,0,1:T(8,128)(2,1)}) fusion(f32[512,16,16]{2,1,0:T(8,128)} %reshape.2450), kind=kLoop, calls=%fused_computation.263 | loop fusion | flops 2359296 | bytes 1835008 | tf_op jit(solution)/shard_map/stack | solution.py:31
  167.2 2.7 copy.64
  170.7 3.1 copy.65
  173.8 3.1 copy.66
  189.9 2.6 reshape.2451
  192.5 33.9 %fusion.45 = (bf16[512,1,16,16]{3,2,0,1:T(8,128)(2,1)S(1)}, bf16[512,1,16,16]{3,2,0,1:T(8,128)(2,1)}, bf16[512,1,16,16]{3,2,0,1:T(8,128)(2,1)}, bf16[512,1,16,16]{3,2,0,1:T(8,128)(2,1)}, bf16[512,1,16,16]{3,2,0,1:T(8,128)(2,1)}) fusion(f32[512,16,16]{2,1,0:T(8,128)} %reshape.2451), kind=kLoop, calls=%fused_computation.262 | loop fusion | flops 2359296 | bytes 1835008 | tf_op jit(solution)/shard_map/stack | solution.py:31
  229.6 3.1 copy.73
  232.7 3.1 copy.74
  235.8 3.1 copy.75
  243.9 34.3 %fusion.44 = (bf16[512,1,16,16]{3,2,0,1:T(8,128)(2,1)S(1)}, bf16[512,1,16,16]{3,2,0,1:T(8,128)(2,1)}, bf16[512,1,16,16]{3,2,0,1:T(8,128)(2,1)}, bf16[512,1,16,16]{3,2,0,1:T(8,128)(2,1)}, bf16[512,1,16,16]{3,2,0,1:T(8,128)(2,1)}) fusion(f32[512,16,16]{2,1,0:T(8,128)} %reshape.2452), kind=kLoop, calls=%fused_computation.261 | loop fusion | flops 2359296 | bytes 1835008 | tf_op jit(solution)/shard_map/stack | solution.py:31
  296.7 11.0 %while.48 = (s32[]{:T(128)}, f32[2,5,512]{2,1,0:T(8,128)S(1)}, s32[2,512]{1,0:T(2,128)S(1)}, f32[2,2,512]{2,1,0:T(2,128)S(1)}, s32[2,512]{1,0:T(2,128)S(1)}, /*i...) while((s32[]{:T(128)}, f32[2,5,512]{2,1,0:T(8,128)S(1)}, s32[2,512]{1,0:T(2,128)S(1)}, ...), condition=%wide.region_1.2_spmd, body=%wide.region_0.1_spmd.sunk | while | flops 674105344 | bytes 8749185 | solution.py:201
  307.8 3.8 fusion.134
  311.5 6.5 %gather_fusion.2 = f32[1024,512]{1,0:T(8,128)} fusion(f32[512,512]{1,0:T(8,128)} %bitcast.278, s32[1024]{0:T(1024)S(1)} %get-tuple-element.791), kind=kCustom, calls=%fused_computation.1.clone | custom fusion | bytes 4198400 | tf_op jit(solution)/shard_map/jit(_take)/gather | solution.py:48
  318.0 6.5 %gather_fusion.3 = f32[1024,512]{1,0:T(8,128)} fusion(f32[512,512]{1,0:T(8,128)} %bitcast.279, s32[1024]{0:T(1024)S(1)} %get-tuple-element.790), kind=kCustom, calls=%fused_computation.2.clone | custom fusion | bytes 4198400 | tf_op jit(solution)/shard_map/jit(_take)/gather | solution.py:48
  324.6 6.5 %gather_fusion.4 = f32[1024,512]{1,0:T(8,128)} fusion(f32[512,512]{1,0:T(8,128)} %bitcast.280, s32[1024]{0:T(1024)S(1)} %get-tuple-element.789), kind=kCustom, calls=%fused_computation.3.clone | custom fusion | bytes 4198400 | tf_op jit(solution)/shard_map/jit(_take)/gather | solution.py:48
  331.1 6.5 %gather_fusion.1 = f32[1024,512]{1,0:T(8,128)} fusion(f32[512,512]{1,0:T(8,128)} %bitcast.281, s32[1024]{0:T(1024)S(1)} %get-tuple-element.792), kind=kCustom, calls=%fused_computation.clone | custom fusion | bytes 4198400 | tf_op jit(solution)/shard_map/jit(_take)/gather | solution.py:48
  337.8 9.6 %select_reduce_fusion.56 = (f32[1024]{0:T(1024)S(1)}, f32[1024]{0:T(1024)S(1)}, f32[1024]{0:T(1024)S(1)}, f32[1024]{0:T(1024)S(1)}, f32[1024]{0:T(1024)S(1)}, /*...) fusion(f32[1024,512]{1,0:T(8,128)} %gather_fusion.2, ...), kind=kLoop, calls=%fused_computation.250 | loop fusion | flops 20955136 | bytes 8474624 | tf_op jit(solution)/shard_map/reduce_sum | solution.py:49
  349.2 19.3 %while.49 = (s32[]{:T(128)}, f32[2,5,512]{2,1,0:T(8,128)S(1)}, s32[2,512]{1,0:T(2,128)S(1)}, f32[2,2,512]{2,1,0:T(2,128)S(1)}, s32[2,512]{1,0:T(2,128)S(1)}, /*i...) while((s32[]{:T(128)}, f32[2,5,512]{2,1,0:T(8,128)S(1)}, s32[2,512]{1,0:T(2,128)S(1)}, ...), condition=%wide.region_19.21_spmd, body=%wide.region_18.20_spmd.sunk | while | flops 674105344 | bytes 8749185 | solution.py:201
  349.2 3.9 fusion.151
  358.8 3.9 fusion.151
  368.5 4.9 %gather_fusion.6 = f32[1024,512]{1,0:T(8,128)} fusion(f32[512,512]{1,0:T(8,128)S(1)} %bitcast.274, s32[1024]{0:T(1024)S(1)} %copy-done.30), kind=kCustom, calls=%fused_computation.5.clone | custom fusion | bytes 4198400 | tf_op jit(solution)/shard_map/jit(_take)/gather | solution.py:48
  373.4 4.9 %gather_fusion.7 = f32[1024,512]{1,0:T(8,128)} fusion(f32[512,512]{1,0:T(8,128)S(1)} %bitcast.275, s32[1024]{0:T(1024)S(1)} %copy-done.29), kind=kCustom, calls=%fused_computation.6.clone | custom fusion | bytes 4198400 | tf_op jit(solution)/shard_map/jit(_take)/gather | solution.py:48
  378.3 4.9 %gather_fusion.8 = f32[1024,512]{1,0:T(8,128)} fusion(f32[512,512]{1,0:T(8,128)S(1)} %bitcast.276, s32[1024]{0:T(1024)S(1)} %copy-done.28), kind=kCustom, calls=%fused_computation.7.clone | custom fusion | bytes 4198400 | tf_op jit(solution)/shard_map/jit(_take)/gather | solution.py:48
  383.2 4.9 %gather_fusion.5 = f32[1024,512]{1,0:T(8,128)} fusion(f32[512,512]{1,0:T(8,128)S(1)} %bitcast.277, s32[1024]{0:T(1024)S(1)} %copy-done.27), kind=kCustom, calls=%fused_computation.4.clone | custom fusion | bytes 4198400 | tf_op jit(solution)/shard_map/jit(_take)/gather | solution.py:48
  388.2 9.5 %select_reduce_fusion.40 = (f32[1024]{0:T(1024)S(1)}, f32[1024]{0:T(1024)S(1)}, f32[1024]{0:T(1024)S(1)}, f32[1024]{0:T(1024)S(1)}, f32[1024]{0:T(1024)S(1)}, /*...) fusion(f32[1024,512]{1,0:T(8,128)} %gather_fusion.6, ...), kind=kLoop, calls=%fused_computation.230 | loop fusion | flops 20955136 | bytes 8474624 | tf_op jit(solution)/shard_map/reduce_sum | solution.py:49
  398.8 13.8 %while.50 = (s32[]{:T(128)}, f32[2,5,512]{2,1,0:T(8,128)S(1)}, s32[2,512]{1,0:T(2,128)S(1)}, f32[2,2,512]{2,1,0:T(2,128)S(1)}, s32[2,512]{1,0:T(2,128)S(1)}, /*i...) while((s32[]{:T(128)}, f32[2,5,512]{2,1,0:T(8,128)S(1)}, s32[2,512]{1,0:T(2,128)S(1)}, ...), condition=%wide.region_37.39_spmd, body=%wide.region_36.38_spmd.sunk | while | flops 674105344 | bytes 8749185 | solution.py:201
  398.8 3.9 fusion.153
  405.7 3.9 fusion.153
  412.6 4.9 %gather_fusion.10 = f32[1024,512]{1,0:T(8,128)} fusion(f32[512,512]{1,0:T(8,128)S(1)} %bitcast.270, s32[1024]{0:T(1024)S(1)} %get-tuple-element.787), kind=kCustom, calls=%fused_computation.9.clone | custom fusion | bytes 4198400 | tf_op jit(solution)/shard_map/jit(_take)/gather | solution.py:48
  417.5 4.9 %gather_fusion.11 = f32[1024,512]{1,0:T(8,128)} fusion(f32[512,512]{1,0:T(8,128)S(1)} %bitcast.271, s32[1024]{0:T(1024)S(1)} %get-tuple-element.786), kind=kCustom, calls=%fused_computation.10.clone | custom fusion | bytes 4198400 | tf_op jit(solution)/shard_map/jit(_take)/gather | solution.py:48
  422.4 4.9 %gather_fusion.12 = f32[1024,512]{1,0:T(8,128)} fusion(f32[512,512]{1,0:T(8,128)S(1)} %bitcast.272, s32[1024]{0:T(1024)S(1)} %get-tuple-element.785), kind=kCustom, calls=%fused_computation.11.clone | custom fusion | bytes 4198400 | tf_op jit(solution)/shard_map/jit(_take)/gather | solution.py:48
  427.4 4.9 %gather_fusion.9 = f32[1024,512]{1,0:T(8,128)} fusion(f32[512,512]{1,0:T(8,128)S(1)} %bitcast.273, s32[1024]{0:T(1024)S(1)} %copy-done.26), kind=kCustom, calls=%fused_computation.8.clone | custom fusion | bytes 4198400 | tf_op jit(solution)/shard_map/jit(_take)/gather | solution.py:48
  432.4 9.6 %select_reduce_fusion.24 = (f32[1024]{0:T(1024)S(1)}, f32[1024]{0:T(1024)S(1)}, f32[1024]{0:T(1024)S(1)}, f32[1024]{0:T(1024)S(1)}, f32[1024]{0:T(1024)S(1)}, /*...) fusion(f32[1024,512]{1,0:T(8,128)} %gather_fusion.10, ...), kind=kLoop, calls=%fused_computation.210 | loop fusion | flops 20955136 | bytes 8474624 | tf_op jit(solution)/shard_map/reduce_sum | solution.py:49
  444.4 12.7 %while.51 = (s32[]{:T(128)}, f32[2,5,512]{2,1,0:T(8,128)S(1)}, s32[2,512]{1,0:T(2,128)}, f32[2,2,512]{2,1,0:T(2,128)S(1)}, s32[2,512]{1,0:T(2,128)}, /*index=5*/...) while((s32[]{:T(128)}, f32[2,5,512]{2,1,0:T(8,128)S(1)}, s32[2,512]{1,0:T(2,128)}, ...), condition=%wide.region_55.57_spmd, body=%wide.region_54.56_spmd.sunk | while | flops 674105344 | bytes 8749185 | solution.py:201
  457.2 3.5 gather_fusion.14
  460.7 4.9 %gather_fusion.15 = f32[1024,512]{1,0:T(8,128)} fusion(f32[512,512]{1,0:T(8,128)S(1)} %bitcast.267, s32[1024]{0:T(1024)S(1)} %copy-done.20), kind=kCustom, calls=%fused_computation.14.clone | custom fusion | bytes 4198400 | tf_op jit(solution)/shard_map/jit(_take)/gather | solution.py:48
  465.6 4.9 %gather_fusion.16 = f32[1024,512]{1,0:T(8,128)} fusion(f32[512,512]{1,0:T(8,128)S(1)} %bitcast.268, s32[1024]{0:T(1024)S(1)} %copy-done.19), kind=kCustom, calls=%fused_computation.15.clone | custom fusion | bytes 4198400 | tf_op jit(solution)/shard_map/jit(_take)/gather | solution.py:48
  470.7 4.9 %gather_fusion.13 = f32[1024,512]{1,0:T(8,128)} fusion(f32[512,512]{1,0:T(8,128)S(1)} %bitcast.269, s32[1024]{0:T(1024)S(1)} %copy-done.18), kind=kCustom, calls=%fused_computation.12.clone | custom fusion | bytes 4198400 | tf_op jit(solution)/shard_map/jit(_take)/gather | solution.py:48
  476.0 9.2 %select_reduce_fusion.8 = (f32[1024]{0:T(1024)S(1)}, f32[1024]{0:T(1024)S(1)}, f32[1024]{0:T(1024)S(1)}, f32[1024]{0:T(1024)S(1)}, f32[1024]{0:T(1024)S(1)}, /*i...) fusion(f32[1024,512]{1,0:T(8,128)S(1)} %gather_fusion.14, ...), kind=kLoop, calls=%fused_computation.190 | loop fusion | flops 20955136 | bytes 8474624 | tf_op jit(solution)/shard_map/reduce_sum | solution.py:49
  (320 shorter events, 128.4 us)
Async XLA Ops:
  0.6 24.1 %copy-start = (bf16[1,1024,256]{2,1,0:T(8,128)(2,1)S(1)}, bf16[1,1024,256]{2,1,0:T(8,128)(2,1)}, u32[]{:S(2)}) copy-start(bf16[1,1024,256]{2,1,0:T(8,128)(2,1)} %param.23) | copy-start | bytes 1572868
  2.2 21.1 %all-to-all-start = ((s32[128,1,16]{2,1,0:T(1,128)}), s32[128,1,16]{2,1,0:T(1,128)S(1)}, u32[]{:S(2)}, u32[]{:S(2)}) async-start(s32[128,1,16]{2,1,0:T(1,128)} %bitcast.38), calls=%async_computation | async-start | bytes 131072 | tf_op jit(solution)/shard_map/all_to_all | solution.py:154
  32.3 11.3 %copy-start.5 = (f32[2,1024]{1,0:T(2,128)S(1)}, f32[2,1024]{1,0:T(2,128)}, u32[]{:S(2)}) copy-start(f32[2,1024]{1,0:T(2,128)} %param.29) | copy-start | bytes 24580
  32.3 11.3 %copy-start.11 = (s32[4,1024]{1,0:T(4,128)S(1)}, s32[4,1024]{1,0:T(4,128)}, u32[]{:S(2)}) copy-start(s32[4,1024]{1,0:T(4,128)} %param.26) | copy-start | bytes 49156
  32.3 29.9 %copy-start.12 = (f32[16,512]{1,0:T(8,128)S(1)}, f32[16,512]{1,0:T(8,128)}, u32[]{:S(2)}) copy-start(f32[16,512]{1,0:T(8,128)} %param.22) | copy-start | bytes 98308
  33.5 28.6 %all-to-all-start.1 = ((bf16[128,16,256]{2,1,0:T(8,128)(2,1)}), bf16[128,16,256]{2,1,0:T(8,128)(2,1)S(1)}, u32[]{:S(2)}, u32[]{:S(2)}) async-start(bf16[128,16,256]{2,1,0:T(8,128)(2,1)} %broadcast_select_fusion), calls=%async_computation.1 | async-start | bytes 2097152 | tf_op jit(solution)/shard_map/all_to_all | solution.py:164
  64.7 243.1 %all-to-all-start.2 = ((f32[128,16,512]{2,1,0:T(8,128)}), f32[128,16,512]{2,1,0:T(8,128)}, u32[]{:S(2)}, u32[]{:S(2)}) async-start(f32[128,16,512]{2,1,0:T(8,128)} %stack.128), calls=%async_computation.2 | async-start | bytes 8388608 | tf_op jit(solution)/shard_map/all_to_all | solution.py:14
  124.1 6.6 %copy-start.2 = (f32[32,16,256]{2,1,0:T(8,128)S(1)}, f32[32,16,256]{2,1,0:T(8,128)}, u32[]{:S(2)}) copy-start(f32[32,16,256]{2,1,0:T(8,128)} %get-tuple-element.623) | copy-start | bytes 1572868
  243.9 34.3 %copy-start.3 = (bf16[512,5,16,16]{0,3,2,1:T(8,128)(2,1)S(1)}, bf16[512,5,16,16]{0,3,2,1:T(8,128)(2,1)}, u32[]{:S(2)}) copy-start(bf16[512,5,16,16]{0,3,2,1:T(8,128)(2,1)} %constant_dynamic-update-slice_fusion.14) | copy-start | bytes 3932164
  331.1 6.6 %copy-start.31 = (s32[1024]{0:T(1024)S(1)}, s32[1024]{0:T(1024)}, u32[]{:S(2)}) copy-start(s32[1024]{0:T(1024)} %get-tuple-element.778) | copy-start | bytes 12292
  331.1 6.6 %copy-start.32 = (s32[1024]{0:T(1024)S(1)}, s32[1024]{0:T(1024)}, u32[]{:S(2)}) copy-start(s32[1024]{0:T(1024)} %get-tuple-element.779) | copy-start | bytes 12292
  331.1 6.6 %copy-start.33 = (s32[1024]{0:T(1024)S(1)}, s32[1024]{0:T(1024)}, u32[]{:S(2)}) copy-start(s32[1024]{0:T(1024)} %get-tuple-element.780) | copy-start | bytes 12292
  331.1 6.6 %copy-start.61 = (pred[1024]{0:T(1024)(128)(4,1)S(1)}, pred[1024]{0:T(1024)(128)(4,1)}, u32[]{:S(2)}) copy-start(pred[1024]{0:T(1024)(128)(4,1)} %get-tuple-element.551) | copy-start | bytes 3076
  331.1 6.6 %copy-start.62 = (pred[1024]{0:T(1024)(128)(4,1)S(1)}, pred[1024]{0:T(1024)(128)(4,1)}, u32[]{:S(2)}) copy-start(pred[1024]{0:T(1024)(128)(4,1)} %get-tuple-element.774) | copy-start | bytes 3076
  331.1 6.6 %copy-start.63 = (pred[1024]{0:T(1024)(128)(4,1)S(1)}, pred[1024]{0:T(1024)(128)(4,1)}, u32[]{:S(2)}) copy-start(pred[1024]{0:T(1024)(128)(4,1)} %get-tuple-element.775) | copy-start | bytes 3076
  331.1 6.6 %copy-start.64 = (pred[1024]{0:T(1024)(128)(4,1)S(1)}, pred[1024]{0:T(1024)(128)(4,1)}, u32[]{:S(2)}) copy-start(pred[1024]{0:T(1024)(128)(4,1)} %get-tuple-element.776) | copy-start | bytes 3076
  337.7 10.0 %copy-start.38 = (f32[1,1024]{1,0:T(1,128)S(1)}, f32[1,1024]{1,0:T(1,128)}, u32[]{:S(2)}) copy-start(f32[1,1024]{1,0:T(1,128)} %get-tuple-element.548) | copy-start | bytes 12292
  337.7 10.0 %copy-start.39 = (f32[1,1024]{1,0:T(1,128)S(1)}, f32[1,1024]{1,0:T(1,128)}, u32[]{:S(2)}) copy-start(f32[1,1024]{1,0:T(1,128)} %get-tuple-element.714) | copy-start | bytes 12292
  337.7 10.0 %copy-start.40 = (f32[1,1024]{1,0:T(1,128)S(1)}, f32[1,1024]{1,0:T(1,128)}, u32[]{:S(2)}) copy-start(f32[1,1024]{1,0:T(1,128)} %get-tuple-element.715) | copy-start | bytes 12292
  337.7 10.0 %copy-start.41 = (f32[1,1024]{1,0:T(1,128)S(1)}, f32[1,1024]{1,0:T(1,128)}, u32[]{:S(2)}) copy-start(f32[1,1024]{1,0:T(1,128)} %get-tuple-element.716) | copy-start | bytes 12292
  337.7 10.0 %copy-start.45 = (f32[5]{0:T(128)S(1)}, f32[5]{0:T(128)}, u32[]{:S(2)}) copy-start(f32[5]{0:T(128)} %constant.668.clone) | copy-start | bytes 64
  337.8 10.7 %copy-start.34 = (s32[4,1024]{1,0:T(4,128)S(1)}, s32[4,1024]{1,0:T(4,128)}, u32[]{:S(2)}) copy-start(s32[4,1024]{1,0:T(4,128)} %param.28) | copy-start | bytes 49156
  349.2 19.3 %copy-start.30 = (s32[1024]{0:T(1024)S(1)}, s32[1024]{0:T(1024)}, u32[]{:S(2)}) copy-start(s32[1024]{0:T(1024)} %get-tuple-element.760) | copy-start | bytes 12292
  388.2 9.8 %copy-start.43 = (f32[1,1024]{1,0:T(1,128)S(1)}, f32[1,1024]{1,0:T(1,128)}, u32[]{:S(2)}) copy-start(f32[1,1024]{1,0:T(1,128)} %get-tuple-element.543) | copy-start | bytes 12292
  388.2 9.8 %copy-start.46 = (f32[5]{0:T(128)S(1)}, f32[5]{0:T(128)}, u32[]{:S(2)}) copy-start(f32[5]{0:T(128)} %constant.668.clone) | copy-start | bytes 64
  432.4 9.9 %copy-start.44 = (f32[1,1024]{1,0:T(1,128)S(1)}, f32[1,1024]{1,0:T(1,128)}, u32[]{:S(2)}) copy-start(f32[1,1024]{1,0:T(1,128)} %get-tuple-element.538) | copy-start | bytes 12292
  432.4 9.9 %copy-start.47 = (f32[5]{0:T(128)S(1)}, f32[5]{0:T(128)}, u32[]{:S(2)}) copy-start(f32[5]{0:T(128)} %constant.668.clone) | copy-start | bytes 64
  432.4 12.0 %copy-start.4 = (bf16[512,1280]{1,0:T(8,128)(2,1)S(1)}, bf16[512,1280]{1,0:T(8,128)(2,1)}, u32[]{:S(2)}) copy-start(bf16[512,1280]{1,0:T(8,128)(2,1)} %copy.85) | copy-start | bytes 3932164
  444.4 12.8 %copy-start.21 = (s32[1024]{0:T(1024)S(1)}, s32[1024]{0:T(1024)}, u32[]{:S(2)}) copy-start(s32[1024]{0:T(1024)} %get-tuple-element.738) | copy-start | bytes 12292
  470.5 5.1 %copy-start.6 = (f32[4,1024]{1,0:T(4,128)S(1)}, f32[4,1024]{1,0:T(4,128)}, u32[]{:S(2)}) copy-start(f32[4,1024]{1,0:T(4,128)} %constant.666.clone.1) | copy-start | bytes 49156
  470.5 5.1 %copy-start.7 = (f32[1,1024]{1,0:T(1,128)S(1)}, f32[1,1024]{1,0:T(1,128)}, u32[]{:S(2)}) copy-start(f32[1,1024]{1,0:T(1,128)} %get-tuple-element.637) | copy-start | bytes 12292
  470.6 5.1 %copy-start.8 = (f32[1,1024]{1,0:T(1,128)S(1)}, f32[1,1024]{1,0:T(1,128)}, u32[]{:S(2)}) copy-start(f32[1,1024]{1,0:T(1,128)} %get-tuple-element.638) | copy-start | bytes 12292
  470.6 5.0 %copy-start.9 = (f32[1,1024]{1,0:T(1,128)S(1)}, f32[1,1024]{1,0:T(1,128)}, u32[]{:S(2)}) copy-start(f32[1,1024]{1,0:T(1,128)} %get-tuple-element.639) | copy-start | bytes 12292
  470.6 5.1 %copy-start.35 = (f32[4,1024]{1,0:T(4,128)S(1)}, f32[4,1024]{1,0:T(4,128)}, u32[]{:S(2)}) copy-start(f32[4,1024]{1,0:T(4,128)} %constant.667.clone.1) | copy-start | bytes 49156
  470.6 5.2 %copy-start.36 = (f32[1,1024]{1,0:T(1,128)S(1)}, f32[1,1024]{1,0:T(1,128)}, u32[]{:S(2)}) copy-start(f32[1,1024]{1,0:T(1,128)} %get-tuple-element.532) | copy-start | bytes 12292
  470.6 5.2 %copy-start.37 = (f32[1,1024]{1,0:T(1,128)S(1)}, f32[1,1024]{1,0:T(1,128)}, u32[]{:S(2)}) copy-start(f32[1,1024]{1,0:T(1,128)} %get-tuple-element.533) | copy-start | bytes 12292
  470.6 5.2 %copy-start.14 = (s32[1024]{0:T(1024)S(1)}, s32[1024]{0:T(1024)}, u32[]{:S(2)}) copy-start(s32[1024]{0:T(1024)} %get-tuple-element.744) | copy-start | bytes 12292
  470.6 5.2 %copy-start.15 = (s32[1024]{0:T(1024)S(1)}, s32[1024]{0:T(1024)}, u32[]{:S(2)}) copy-start(s32[1024]{0:T(1024)} %get-tuple-element.745) | copy-start | bytes 12292
  470.6 5.2 %copy-start.16 = (s32[1024]{0:T(1024)S(1)}, s32[1024]{0:T(1024)}, u32[]{:S(2)}) copy-start(s32[1024]{0:T(1024)} %get-tuple-element.746) | copy-start | bytes 12292
  470.6 5.2 %copy-start.17 = (s32[1024]{0:T(1024)S(1)}, s32[1024]{0:T(1024)}, u32[]{:S(2)}) copy-start(s32[1024]{0:T(1024)} %get-tuple-element.747) | copy-start | bytes 12292
  470.7 5.2 %copy-start.49 = (pred[1024]{0:T(1024)(128)(4,1)S(1)}, pred[1024]{0:T(1024)(128)(4,1)}, u32[]{:S(2)}) copy-start(pred[1024]{0:T(1024)(128)(4,1)} %get-tuple-element.534) | copy-start | bytes 3076
  470.7 5.2 %copy-start.50 = (pred[1024]{0:T(1024)(128)(4,1)S(1)}, pred[1024]{0:T(1024)(128)(4,1)}, u32[]{:S(2)}) copy-start(pred[1024]{0:T(1024)(128)(4,1)} %get-tuple-element.741) | copy-start | bytes 3076
  470.7 5.2 %copy-start.51 = (pred[1024]{0:T(1024)(128)(4,1)S(1)}, pred[1024]{0:T(1024)(128)(4,1)}, u32[]{:S(2)}) copy-start(pred[1024]{0:T(1024)(128)(4,1)} %get-tuple-element.742) | copy-start | bytes 3076
  470.7 5.2 %copy-start.52 = (pred[1024]{0:T(1024)(128)(4,1)S(1)}, pred[1024]{0:T(1024)(128)(4,1)}, u32[]{:S(2)}) copy-start(pred[1024]{0:T(1024)(128)(4,1)} %get-tuple-element.743) | copy-start | bytes 3076
  475.9 9.5 %copy-start.42 = (f32[1,1024]{1,0:T(1,128)S(1)}, f32[1,1024]{1,0:T(1,128)}, u32[]{:S(2)}) copy-start(f32[1,1024]{1,0:T(1,128)} %get-tuple-element.531) | copy-start | bytes 12292
  475.9 9.5 %copy-start.48 = (f32[5]{0:T(128)S(1)}, f32[5]{0:T(128)}, u32[]{:S(2)}) copy-start(f32[5]{0:T(128)} %constant.668.clone) | copy-start | bytes 64
  475.9 9.6 %copy-start.13 = (f32[2,1024]{1,0:T(2,128)S(1)}, f32[2,1024]{1,0:T(2,128)}, u32[]{:S(2)}) copy-start(f32[2,1024]{1,0:T(2,128)} %get-tuple-element.537) | copy-start | bytes 24580
  476.0 10.9 %copy-start.1 = (bf16[1,1024,256]{2,1,0:T(8,128)(2,1)S(1)}, bf16[1,1024,256]{2,1,0:T(8,128)(2,1)}, u32[]{:S(2)}) copy-start(bf16[1,1024,256]{2,1,0:T(8,128)(2,1)} %param.23) | copy-start | bytes 1572868
  (20 other events, 97.8 us)
